TPU v7x, 128 devices: a whole 4x4x4 slice. The times are simulated.
128 devices in a mesh: row: 16 (over y_lo, z, core), col: 8 (over x, y_hi).
Axes of the slice: x: 4, y: 4 (y_hi: 2, y_lo: 2; y = y_hi * 2 + y_lo), z: 4, core: 2. Of those that a mesh axis runs over, the one named last changes fastest.
Arguments:
- hidden_in: bfloat16 [8192, 2048], P('row'), may hold values from -6 to 6
- gain_attn: float32 [2048], replicated, may hold values from 0.1 to 1.9
- gain_mlp: float32 [2048], replicated, may hold values from 0.1 to 1.9
- w_qkv: bfloat16 [2048, 3, 2048], P('row', None, 'col'), may hold values from -0.25 to 0.25
- w_up: bfloat16 [2048, 8192], P('row', 'col'), may hold values from -0.25 to 0.25
- w_out: bfloat16 [2048, 2048], P('col', 'row'), may hold values from -0.125 to 0.125
- w_down: bfloat16 [8192, 2048], P('col', 'row'), may hold values from -0.0625 to 0.0625
- prefix_cache: bfloat16 [128, 128, 2, 2048], P('row', None, None, 'col'), may hold values from -136 to 136, as said below
- suffix_lengths: int32 [64], replicated, may hold values from 1 to 512, 8192 in all
- cached_lengths: int32 [64], replicated, may hold values from 1 to 8192, as said below
- request_group: int32 [64], replicated, may hold values from 0 to 1
- page_table: int32 [128], replicated, may hold values from 0 to 127, each once
Outputs:
- hidden_out: bfloat16 [8192, 2048], P('row', 'col')
- suffix_keys: bfloat16 [8192, 2048], P('row', 'col')
- suffix_values: bfloat16 [8192, 2048], P('row', 'col')
Inputs may be any that keep to these rules, and one draw needn't show every extreme that they name: `suffix_lengths`: the lengths sum to 8192; some request has exactly 512 tokens. `cached_lengths`: some request reuses all 8192 tokens of its prefix. `page_table`: each slot appears once; slot s is held by index s // 8 of row. `prefix_cache`: keys and values of the prefix pages.
All inputs are finite; a program needn't handle non-finite values.
Results may differ from a plain program's by a relative error of at most 0.02.
Values may be sent and summed in bfloat16 or wider, within the bound.
A program may use at most 128 MiB of HBM per device.

v0:
```python
import math
import jax
import jax.numpy as jnp
from jax import lax
from jax.sharding import PartitionSpec as P

HD = 256
ROT = 64
PAGE = 128
GROUPS = 2
very_low = -1e30
norm_epsilon = 1e-05


def from_behind(block, axis, distance):
    devices = range(lax.axis_size(axis))
    route = [(i - distance, i) for i in devices if i - distance in devices]
    return lax.ppermute(block, axis, route)


def layer_normalize(values):
    floats = values.astype(jnp.float32)
    average = jnp.mean(floats, -1, keepdims=True)
    centered = floats - average
    spread = jnp.mean(centered * centered, -1, keepdims=True)
    return centered * lax.rsqrt(spread + norm_epsilon)


def rotary(vectors, position):
    half_rot = ROT // 2
    exponent = jnp.arange(half_rot, dtype=jnp.float32) * (2.0 / ROT)
    frequency = 10000.0 ** (-exponent)
    angles = position.astype(jnp.float32)[:, None] * frequency[None, :]
    cosine = jnp.concatenate([jnp.cos(angles), jnp.cos(angles)], 1)[:, None, :]
    sine = jnp.concatenate([jnp.sin(angles), jnp.sin(angles)], 1)[:, None, :]
    rotated = vectors[..., :ROT]
    turned = jnp.concatenate([-rotated[..., half_rot:], rotated[..., :half_rot]], -1)
    return jnp.concatenate([rotated * cosine + turned * sine, vectors[..., ROT:]], -1)


def token_table(suffix_lengths, cached_lengths, request_group, count):
    starts = jnp.cumsum(suffix_lengths, dtype=jnp.int32) - suffix_lengths
    token_ids = jnp.arange(count, dtype=jnp.int32)
    request = (
        jnp.sum((starts[None, :] <= token_ids[:, None]).astype(jnp.int32), 1, dtype=jnp.int32) - 1
    )
    onehot = (
        request[:, None] == jnp.arange(suffix_lengths.shape[0], dtype=jnp.int32)[None, :]
    ).astype(jnp.int32)
    begin = jnp.sum(onehot * starts[None, :], 1, dtype=jnp.int32)
    limit = jnp.sum(onehot * cached_lengths[None, :], 1, dtype=jnp.int32)
    group_of = jnp.sum(onehot * request_group[None, :], 1, dtype=jnp.int32)
    return (request, limit + token_ids - begin, group_of, limit)


def partial_softmax(scores, visible, value_block):
    allowed = visible[None, :, :]
    peak = jnp.max(jnp.where(allowed, scores, very_low), -1)
    weights = jnp.where(allowed, jnp.exp(scores - peak[..., None]), 0.0)
    total = jnp.sum(weights, -1)
    mixed = jnp.einsum(
        "hqk,khe->qhe",
        weights.astype(jnp.bfloat16),
        value_block,
        preferred_element_type=jnp.float32,
    )
    return (peak, total, mixed)


def combine(earlier, later):
    peak = jnp.maximum(earlier[0], later[0])
    scale_one = jnp.exp(earlier[0] - peak)
    scale_two = jnp.exp(later[0] - peak)
    total = earlier[1] * scale_one + later[1] * scale_two
    mixed = earlier[2] * scale_one.T[:, :, None] + later[2] * scale_two.T[:, :, None]
    return (peak, total, mixed)


def prefix_fold(running, cache_rows, query_block, query_group, query_limit, page_table):
    count = cache_rows.shape[0]
    stride = math.gcd(count, 8)
    heads_here = query_block.shape[1]
    per_prefix = page_table.shape[0] // GROUPS
    table_index = jnp.arange(page_table.shape[0], dtype=jnp.int32)

    def advance(turn_index, inner):
        block_rows = lax.dynamic_slice_in_dim(cache_rows, turn_index * stride, stride, 0)
        slots = turn_index * stride + jnp.arange(stride, dtype=jnp.int32)
        logical = jnp.sum(
            table_index[None, :] * (page_table[None, :] == slots[:, None]).astype(jnp.int32),
            1,
            dtype=jnp.int32,
        )
        key_group = jnp.repeat(logical // per_prefix, PAGE)
        key_position = (
            (logical % per_prefix)[:, None] * PAGE + jnp.arange(PAGE, dtype=jnp.int32)[None, :]
        ).reshape(-1)
        key_block = block_rows[:, :, 0].reshape(stride * PAGE, heads_here, HD)
        value_block = block_rows[:, :, 1].reshape(stride * PAGE, heads_here, HD)
        visible = (key_group[None, :] == query_group[:, None]) & (
            key_position[None, :] < query_limit[:, None]
        )
        scores = jnp.einsum(
            "qhe,khe->hqk", query_block, key_block, preferred_element_type=jnp.float32
        )
        return combine(inner, partial_softmax(scores, visible, value_block))

    return lax.fori_loop(0, count // stride, advance, running)


def body(
    hidden_in,
    gain_attn,
    gain_mlp,
    w_qkv,
    w_up,
    w_out,
    w_down,
    prefix_cache,
    suffix_lengths,
    cached_lengths,
    request_group,
    page_table,
):
    row_count = hidden_in.shape[0]
    model_width = hidden_in.shape[1]
    row_total = lax.axis_size("row")
    col_total = lax.axis_size("col")
    row_place = lax.axis_index("row")
    col_place = lax.axis_index("col")
    head_width = w_qkv.shape[2]
    heads_here = head_width // HD
    normed = layer_normalize(hidden_in)
    attn_in = (normed * gain_attn).astype(jnp.bfloat16)
    mlp_in = (normed * gain_mlp).astype(jnp.bfloat16)
    rows_here = w_qkv.shape[0]
    qkv_columns = 3 * head_width
    joined = jnp.concatenate([w_qkv.reshape(rows_here, qkv_columns), w_up], 1)
    joined = lax.all_gather(joined, "row", axis=0, tiled=True)
    qkv_all = joined[:, :qkv_columns].reshape(model_width, 3, head_width)
    projected = jnp.einsum("td,dkh->tkh", attn_in, qkv_all, preferred_element_type=jnp.float32)
    up_sum = jnp.dot(mlp_in, joined[:, qkv_columns:], preferred_element_type=jnp.float32)
    token_total = row_total * row_count
    request_all, position_all, group_all, limit_all = token_table(
        suffix_lengths, cached_lengths, request_group, token_total
    )
    first_row = row_place * row_count
    local_request = lax.dynamic_slice_in_dim(request_all, first_row, row_count, 0)
    local_position = lax.dynamic_slice_in_dim(position_all, first_row, row_count, 0)
    local_group = lax.dynamic_slice_in_dim(group_all, first_row, row_count, 0)
    local_limit = lax.dynamic_slice_in_dim(limit_all, first_row, row_count, 0)
    projected = projected.reshape(row_count, 3, heads_here, HD)
    queries = (rotary(projected[:, 0], local_position) * HD ** (-0.5)).astype(jnp.bfloat16)
    keys_flat = (
        rotary(projected[:, 1], local_position).astype(jnp.bfloat16).reshape(row_count, head_width)
    )
    values_flat = projected[:, 2].astype(jnp.bfloat16).reshape(row_count, head_width)
    pair_rows = jnp.stack([keys_flat, values_flat], 1)
    previous = from_behind(pair_rows, "row", 1)
    window = jnp.concatenate([previous, pair_rows], 0)
    window_ids = first_row - row_count + jnp.arange(2 * row_count, dtype=jnp.int32)
    padded_request = jnp.concatenate([jnp.full((row_count,), -1, jnp.int32), request_all], 0)
    window_request = lax.dynamic_slice_in_dim(padded_request, first_row, 2 * row_count, 0)
    token_ids = first_row + jnp.arange(row_count, dtype=jnp.int32)
    visible = (window_request[None, :] == local_request[:, None]) & (
        window_ids[None, :] <= token_ids[:, None]
    )
    window_keys = window[:, 0].reshape(2 * row_count, heads_here, HD)
    window_values = window[:, 1].reshape(2 * row_count, heads_here, HD)
    scores = jnp.einsum("qhe,khe->hqk", queries, window_keys, preferred_element_type=jnp.float32)
    suffix_state = partial_softmax(scores, visible, window_values)
    start_state = (
        jnp.full((heads_here, row_count), very_low, jnp.float32),
        jnp.zeros((heads_here, row_count), jnp.float32),
        jnp.zeros((row_count, heads_here, HD), jnp.float32),
    )
    prefix_state = prefix_fold(
        start_state,
        lax.all_gather(prefix_cache, "row", axis=0, tiled=True),
        queries,
        local_group,
        local_limit,
        page_table,
    )
    final = combine(prefix_state, suffix_state)
    attention = (
        (final[2] / final[1].T[:, :, None]).astype(jnp.bfloat16).reshape(row_count, head_width)
    )
    activated = jax.nn.gelu(up_sum, approximate=False).astype(jnp.bfloat16)
    out_rows = w_out.shape[0]
    joined = jnp.concatenate([w_out.T, w_down.T], 1)
    joined = lax.all_gather(joined, "row", axis=0, tiled=True)
    contribution = jnp.einsum(
        "th,dh->td", attention, joined[:, :out_rows], preferred_element_type=jnp.float32
    ) + jnp.einsum("tf,df->td", activated, joined[:, out_rows:], preferred_element_type=jnp.float32)
    summed = lax.psum_scatter(
        contribution.astype(jnp.bfloat16), "col", scatter_dimension=1, tiled=True
    ).astype(jnp.float32)
    share = model_width // col_total
    residual = lax.dynamic_slice_in_dim(hidden_in, col_place * share, share, 1).astype(jnp.float32)
    return ((residual + summed).astype(jnp.bfloat16), keys_flat, values_flat)


def solution(mesh):
    in_specs = (
        P("row", None),
        P(),
        P(),
        P("row", None, "col"),
        P("row", "col"),
        P("col", "row"),
        P("col", "row"),
        P("row", None, None, "col"),
        P(),
        P(),
        P(),
        P(),
    )
    out_specs = (P("row", "col"), P("row", "col"), P("row", "col"))
    return jax.shard_map(body, mesh=mesh, in_specs=in_specs, out_specs=out_specs, check_vma=False)
```

profile of v0, /device:TPU:0, one launch (start us, length us, event | category | flops | bytes accessed | tf_op | source)
XLA Modules:
  0.0 390.6 jit_solution(15160892057513650524)
XLA Ops:
  8.6 1.8 pad_maximum_fusion.1
  15.8 44.4 %all-gather.6.cloned.1.call-done = bf16[2048,1792]{1,0:T(8,128)(2,1)} async-done(((bf16[128,1792]{1,0:T(8,128)(2,1)}), bf16[2048,1792]{1,0:T(8,128)(2,1)}) %all-gather.6.cloned.1.call-update) | async-done | bytes 7340048 | tf_op jit(solution)/shard_map/all_gather | solution.py:139
  60.2 1.9 slice-done
  62.1 3.0 copy.37
  65.1 4.5 %fusion.40 = f32[512,3,256]{0,2,1:T(8,128)S(1)} fusion(bf16[2048,3,256]{0,2,1:T(8,128)(2,1)} %bitcast.156, bf16[512,2048]{1,0:T(8,128)(2,1)} %param.14, f32[2048]{0:T(1024)S(1)} %copy-done.15, f32[512]{0:T(512)S(1)} %add_rsqrt_fusion, f32[512]{0:T(512)S(1)} %broadcast_multiply_fusion), kind=kOutput, calls=%fused_computation.61 | convolution fusion | flops 1615855616 | bytes 6828032 | tf_op jit(solution)/shard_map/td,dkh->tkh/dot_general | solution.py:141
  72.1 3.0 collective-permute-start
  75.0 39.2 %all-gather.8.cloned.1.call-done = bf16[2048,1280]{0,1:T(8,128)(2,1)} async-done(((bf16[128,1280]{0,1:T(8,128)(2,1)}), bf16[2048,1280]{0,1:T(8,128)(2,1)}) %all-gather.8.cloned.1.call-update) | async-done | bytes 5242896 | tf_op jit(solution)/shard_map/all_gather | solution.py:192
  114.3 14.3 %fusion.31 = f32[512,2048]{1,0:T(8,128)} fusion(bf16[2048,1280]{0,1:T(8,128)(2,1)} %all-gather.8.cloned.1.call-done, bf16[2048,1792]{1,0:T(8,128)(2,1)} %all-gather.6.cloned.1.call-done, bf16[512,2048]{1,0:T(8,128)(2,1)S(1)} %copy-done.1, f32[2048]{0:T(1024)S(1)} %copy-done.16, f32[512]{0:T(512)S(1)} %add_rsqrt_fusion, f32[512]{0:T(512)S(1)} %broadcast_multiply_fusion), kind=kOutput, calls=%fused_computation.51 | convolution fusion | flops 4334288896 | bytes 14692352 | tf_op jit(solution)/shard_map/tf,df->td/dot_general | solution.py:195
  132.7 1.3 copy-done.2
  134.8 73.3 %all-gather.4.cloned.1.call-done = bf16[128,128,2,256]{3,1,0,2:T(8,128)(2,1)} async-done(((bf16[8,128,2,256]{3,1,0,2:T(8,128)(2,1)}), bf16[128,128,2,256]{3,1,0,2:T(8,128)(2,1)}) %all-gather.4.cloned.1.call-update) | async-done | bytes 16777232 | tf_op jit(solution)/shard_map/all_gather | solution.py:179
  208.1 91.4 %while.20 = (s32[]{:T(128)}, f32[1,512]{1,0:T(1,128)S(1)}, f32[1,512]{1,0:T(1,128)S(1)}, f32[512,1,256]{0,2,1:T(8,128)}, s32[128]{0:T(128)S(1)}, /*index=5*/s32[...) while((s32[]{:T(128)}, f32[1,512]{1,0:T(1,128)S(1)}, ...), condition=%wide.region_11.12_spmd.clone, body=%wide.region_7.0_spmd.clone.sunk | while | flops 546315392 | bytes 11871218 | solution.py:108
  208.1 1.3 constant_dynamic-slice_fusion.3
  211.1 1.7 fusion.186
  212.8 1.3 constant_dynamic-slice_fusion.3
  215.9 2.7 fusion.186
  221.6 2.7 fusion.186
  227.4 2.7 fusion.186
  233.2 2.7 fusion.186
  239.0 2.7 fusion.186
  244.7 2.7 fusion.186
  250.5 2.7 fusion.186
  256.3 2.7 fusion.186
  262.1 2.7 fusion.186
  267.8 2.7 fusion.186
  273.6 2.7 fusion.186
  279.4 2.7 fusion.186
  285.2 2.7 fusion.186
  290.9 2.7 fusion.186
  296.7 2.7 fusion.186
  299.5 6.3 %add_convert_fusion = bf16[512,2048]{1,0:T(8,128)(2,1)} fusion(f32[512,2048]{1,0:T(8,128)} %fusion.31, bf16[2048,1280]{0,1:T(8,128)(2,1)} %all-gather.8.cloned.1.call-done, f32[512,1024]{1,0:T(8,128)} %copy-done.2, f32[512]{0:T(512)S(1)} %get-tuple-element.373, s32[1024]{0:T(1024)S(1)} %get-tuple-element.378, s32[1024]{0:T(1024)S(1)} %get-tuple-element.377, ...), kind=kOutput, calls=%fused_computation.55 | convolution fusion | flops 811204608 | bytes 10506240 | tf_op jit(solution)/shard_map/th,dh->td/dot_general | solution.py:193
  307.5 74.7 %reduce-scatter.2.cloned.1.call-done = bf16[512,256]{1,0:T(8,128)(2,1)} async-done(((bf16[512,2048]{1,0:T(8,128)(2,1)}), bf16[512,256]{1,0:T(8,128)(2,1)}) %reduce-scatter.2.cloned.1.call-update) | async-done | bytes 262160 | tf_op jit(solution)/shard_map/reduce_scatter | solution.py:196
  382.3 1.8 add_convert_fusion.1
  (243 shorter events, 61.6 us)
Async XLA Ops:
  7.2 3.3 copy-start.11
  7.2 3.3 copy-start.9
  7.2 4.1 %copy-start.6 = (bf16[8,128,2,256]{3,2,1,0:T(2,128)(2,1)S(1)}, bf16[8,128,2,256]{3,2,1,0:T(2,128)(2,1)}, u32[]{:S(2)}) copy-start(bf16[8,128,2,256]{3,2,1,0:T(2,128)(2,1)} %param.21) | copy-start | bytes 3145732
  7.2 53.0 %all-gather.6.cloned.1.call-start = ((), (), s32[]{:S(2)}) async-start(), calls=%async_computation.2 | async-start | bytes 7798784 | tf_op jit(solution)/shard_map/all_gather | solution.py:139
  10.4 2.2 copy-start.12
  10.4 103.9 %all-gather.8.cloned.1.call-start = ((), (), s32[]{:S(2)}) async-start(), calls=%async_computation.3 | async-start | bytes 5570560 | tf_op jit(solution)/shard_map/all_gather | solution.py:192
  10.5 2.9 copy-start.13
  10.5 2.9 copy-start.14
  11.2 3.2 copy-start
  11.3 196.8 %all-gather.4.cloned.1.call-start = ((), (), s32[]{:S(2)}) async-start(), calls=%async_computation.1 | async-start | bytes 17825792 | tf_op jit(solution)/shard_map/all_gather | solution.py:179
  12.5 369.8 %reduce-scatter.2.cloned.1.call-start = ((), (), s32[]{:S(2)}) async-start(), calls=%async_computation.4 | async-start | bytes 2359296 | tf_op jit(solution)/shard_map/reduce_scatter | solution.py:196
  60.2 1.9 slice-start
  62.1 3.0 copy-start.15
  69.7 44.6 %copy-start.1 = (bf16[512,2048]{1,0:T(8,128)(2,1)S(1)}, bf16[512,2048]{1,0:T(8,128)(2,1)}, u32[]{:S(2)}) copy-start(bf16[512,2048]{1,0:T(8,128)(2,1)} %param.14) | copy-start | bytes 6291460
  69.7 44.5 %copy-start.16 = (f32[2048]{0:T(1024)S(1)}, f32[2048]{0:T(1024)}, u32[]{:S(2)}) copy-start(f32[2048]{0:T(1024)} %param.16) | copy-start | bytes 24580
  72.1 58.4 %collective-permute-start = (bf16[512,2,256]{0,2,1:T(8,128)(2,1)}, bf16[512,2,256]{0,2,1:T(8,128)(2,1)}, u32[]{:S(2)}, u32[]{:S(2)}) collective-permute-start(bf16[512,2,256]{0,2,1:T(8,128)(2,1)} %pad_maximum_fusion), channel_id=1, source_target_pairs={{0,8},{8,16},{16,24},{24,32},{32,40},{40,48},{48,56},{56,64},{64,7... | collective-permute-start | bytes 1572872 | tf_op jit(solution)/shard_map/ppermute | solution.py:18
  128.6 1.9 copy-start.4
  128.6 3.1 copy-start.8
  132.7 75.4 %copy-start.17 = (s32[128]{0:T(128)S(1)}, s32[128]{0:T(128)}, u32[]{:S(2)}) copy-start(s32[128]{0:T(128)} %param.25) | copy-start | bytes 1540
  208.1 1.6 copy-start.10
  212.8 1.6 copy-start.10
  218.6 1.6 copy-start.10
  224.3 1.6 copy-start.10
  230.1 1.6 copy-start.10
  235.9 1.6 copy-start.10
  241.7 1.6 copy-start.10
  247.5 1.6 copy-start.10
  253.2 1.6 copy-start.10
  259.0 1.6 copy-start.10
  276.3 1.6 copy-start.10
  282.1 1.6 copy-start.10
  287.9 1.6 copy-start.10
  (7 other events, 9.6 us)
Sparse Core Ops, SparseCore 0:
  10.5 49.6 all-gather.5
  61.8 52.3 all-gather.7
  115.9 92.0 all-gather.3
  305.9 76.3 reduce-scatter.1
where the time goes:
time: 392 us; the launch traced here: 391 us
  waiting for transfers between devices  232 us (59%)
  matrix products  77.4 us (20%)
  local copies, waits for them, and re-layouts  33.8 us (9%)
  other arithmetic  30.1 us (8%)
  between operations  14 us (4%)
    all_gather x2, waiting for transfers between devices, body(): joined = lax.all_gather(joined, 'row', axis=0, tiled=True)  83.6 us
    reduce_scatter x1, waiting for transfers between devices, body(): lax.psum_scatter(contribution.astype(jnp.bfloat16), 'col', scatter_dimens...  74.7 us
    all_gather x1, waiting for transfers between devices, body(): lax.all_gather(prefix_cache, 'row', axis=0, tiled=True)  73.3 us
    dot_general x16, matrix products, partial_softmax(): jnp.einsum('hqk,khe->qhe', weights.astype(jnp.bfloat16), value_block, pre...  42.5 us
    slice x16, local copies, waits for them, and re-layouts, advance(): value_block = block_rows[:, :, 1].reshape(stride * PAGE, heads_here, HD)  21 us
    dot_general x1, matrix products, body(): jnp.einsum('tf,df->td', activated, joined[:, out_rows:], preferred_elemen...  14.3 us
    reduce_sum x17, other arithmetic, partial_softmax(): total = jnp.sum(weights, -1)  14.2 us
    dot_general x16, matrix products, advance(): jnp.einsum('qhe,khe->hqk', query_block, key_block, preferred_element_type...  9.17 us
  transfers between devices with their start and end apart: 5, of which 4 were waited for; matrix products, arithmetic and copies ran while one was open for 9% of the time, Pallas kernels for 0%

commit v1 on v0

--- a/solution.py
+++ b/solution.py
@@ -174,9 +174,16 @@
         jnp.zeros((heads_here, row_count), jnp.float32),
         jnp.zeros((row_count, heads_here, HD), jnp.float32),
     )
+
+    def fit_tokens_for(frame, axis_name):
+        z2 = lax.all_to_all(
+            jnp.stack(lax.axis_size(axis_name) * [frame]), axis_name, split_axis=0, concat_axis=0
+        )
+        return jnp.concatenate(z2, axis=0)
+
     prefix_state = prefix_fold(
         start_state,
-        lax.all_gather(prefix_cache, "row", axis=0, tiled=True),
+        fit_tokens_for(prefix_cache, "row"),
         queries,
         local_group,
         local_limit,

time: 392 us -> 519 us (1.32)
  waiting for transfers between devices: 232 us -> 333 us
  local copies, waits for them, and re-layouts: 33.8 us -> 53 us
  starting transfers between devices: 3.13 us -> 9.79 us
    all_gather x2, waiting for transfers between devices: 83.6 us -> 260 us  [body(): joined = lax.all_gather(joined, 'row', axis=0, tiled=True)]
    all_gather x1 -> x0, waiting for transfers between devices: 73.3 us -> none  [body(): lax.all_gather(prefix_cache, 'row', axis=0, tiled=True)]
    all_to_all x0 -> x1, local copies, waits for them, and re-layouts: none -> 14.2 us  [fit_tokens_for(): lax.all_to_all(jnp.stack(lax.axis_size(axis_name) * [frame]), axis_name,...]
    all_to_all x0 -> x1, starting transfers between devices: none -> 6.71 us  [fit_tokens_for(): lax.all_to_all(jnp.stack(lax.axis_size(axis_name) * [frame]), axis_name,...]
    another operation x1 -> x2, local copies, waits for them, and re-layouts: 0.1 us -> 6.04 us  [the longest x1 5.94 us: fit_tokens_for(): jnp.stack(lax.axis_size(axis_name) * [frame])]
  transfers between devices with their start and end apart: 5 -> 5, of which waited for: 4 -> 3; matrix products, arithmetic and copies ran while one was open for 9% -> 8% of each run, Pallas kernels for 0% -> 0%
where the time goes in v1:
time: 519 us; the launch traced here: 518 us
  waiting for transfers between devices  333 us (64%)
  matrix products  77.2 us (15%)
  local copies, waits for them, and re-layouts  53 us (10%)
  other arithmetic  30 us (6%)
  between operations  14.1 us (3%)
  starting transfers between devices  9.79 us (2%)
    all_gather x2, waiting for transfers between devices, body(): joined = lax.all_gather(joined, 'row', axis=0, tiled=True)  260 us
    reduce_scatter x1, waiting for transfers between devices, body(): lax.psum_scatter(contribution.astype(jnp.bfloat16), 'col', scatter_dimens...  73.7 us
    dot_general x16, matrix products, partial_softmax(): jnp.einsum('hqk,khe->qhe', weights.astype(jnp.bfloat16), value_block, pre...  42.2 us
    slice x16, local copies, waits for them, and re-layouts, advance(): value_block = block_rows[:, :, 1].reshape(stride * PAGE, heads_here, HD)  21 us
    dot_general x1, matrix products, body(): jnp.einsum('tf,df->td', activated, joined[:, out_rows:], preferred_elemen...  14.3 us
    reduce_sum x17, other arithmetic, partial_softmax(): total = jnp.sum(weights, -1)  14.2 us
    all_to_all x1, local copies, waits for them, and re-layouts, fit_tokens_for(): lax.all_to_all(jnp.stack(lax.axis_size(axis_name) * [frame]), axis_name,...  14.2 us
  transfers between devices with their start and end apart: 5, of which 3 were waited for; matrix products, arithmetic and copies ran while one was open for 8% of the time, Pallas kernels for 0%

profile of v1, /device:TPU:0, one launch (start us, length us, event | category | flops | bytes accessed | tf_op | source)
XLA Modules:
  0.0 517.7 jit_solution(10592641433756815120)
XLA Ops:
  8.5 1.8 pad_maximum_fusion.1
  10.5 5.9 %stack.4 = bf16[16,8,128,2,256]{4,2,1,3,0:T(8,128)(2,1)} broadcast(bf16[8,128,2,256]{3,1,0,2:T(8,128)(2,1)S(1)} %copy.56), dimensions={1,2,3,4} | broadcast | bytes 17825792 | tf_op jit(solution)/shard_map/stack | solution.py:180
  16.5 6.7 %all-to-all-start = ((bf16[16,8,128,2,256]{4,2,1,3,0:T(8,128)(2,1)}), bf16[16,8,128,2,256]{4,2,1,3,0:T(8,128)(2,1)}, u32[]{:S(2)}, u32[]{:S(2)}) async-start(bf16[16,8,128,2,256]{4,2,1,3,0:T(8,128)(2,1)} %stack.4), calls=%async_computation | async-start | bytes 33554432 | tf_op jit(solution)/shard_map/all_to_all | solution.py:179
  27.4 212.1 %all-gather.3.cloned.1.call-done = bf16[2048,1792]{1,0:T(8,128)(2,1)} async-done(((bf16[128,1792]{1,0:T(8,128)(2,1)}), bf16[2048,1792]{1,0:T(8,128)(2,1)}) %all-gather.3.cloned.1.call-update) | async-done | bytes 7340048 | tf_op jit(solution)/shard_map/all_gather | solution.py:139
  239.4 1.9 slice-done
  241.3 3.0 copy.60
  244.3 4.5 fusion.40
  251.2 3.0 collective-permute-start
  254.2 47.4 %all-gather.5.cloned.1.call-done = bf16[2048,1280]{0,1:T(8,128)(2,1)} async-done(((bf16[128,1280]{0,1:T(8,128)(2,1)}), bf16[2048,1280]{0,1:T(8,128)(2,1)}) %all-gather.5.cloned.1.call-update) | async-done | bytes 5242896 | tf_op jit(solution)/shard_map/all_gather | solution.py:199
  301.7 14.3 %fusion.31 = f32[512,2048]{1,0:T(8,128)} fusion(bf16[2048,1280]{0,1:T(8,128)(2,1)} %all-gather.5.cloned.1.call-done, bf16[2048,1792]{1,0:T(8,128)(2,1)} %all-gather.3.cloned.1.call-done, bf16[512,2048]{1,0:T(8,128)(2,1)S(1)} %copy-done.1, f32[2048]{0:T(1024)S(1)} %copy-done.16, f32[512]{0:T(512)S(1)} %add_rsqrt_fusion, f32[512]{0:T(512)S(1)} %broadcast_multiply_fusion), kind=kOutput, calls=%fused_computation.51 | convolution fusion | flops 4334288896 | bytes 14692352 | tf_op jit(solution)/shard_map/tf,df->td/dot_general | solution.py:202
  320.1 1.3 copy-done.2
  322.2 14.2 %copy.57 = bf16[16,8,128,2,256]{4,2,3,1,0:T(8,128)(2,1)} copy(bf16[16,8,128,2,256]{4,2,1,3,0:T(8,128)(2,1)} %all-to-all-done) | data formatting | bytes 33554432 | tf_op jit(solution)/shard_map/all_to_all | solution.py:179
  336.4 91.1 %while.20 = (s32[]{:T(128)}, f32[1,512]{1,0:T(1,128)S(1)}, f32[1,512]{1,0:T(1,128)S(1)}, f32[512,1,256]{0,2,1:T(8,128)}, s32[128]{0:T(128)S(1)}, /*index=5*/s32[...) while((s32[]{:T(128)}, f32[1,512]{1,0:T(1,128)S(1)}, ...), condition=%wide.region_11.12_spmd.clone, body=%wide.region_7.0_spmd.clone.sunk | while | flops 546315392 | bytes 11871218 | solution.py:108
  339.5 1.7 fusion.186
  344.2 2.7 fusion.186
  350.0 2.7 fusion.186
  355.7 2.7 fusion.186
  361.5 2.7 fusion.186
  367.2 2.7 fusion.186
  373.0 2.7 fusion.186
  378.8 2.7 fusion.186
  384.5 2.7 fusion.186
  390.3 2.7 fusion.186
  396.0 2.7 fusion.186
  401.8 2.7 fusion.186
  407.6 2.7 fusion.186
  413.3 2.7 fusion.186
  419.1 2.7 fusion.186
  424.8 2.7 fusion.186
  427.6 6.3 %add_convert_fusion = bf16[512,2048]{1,0:T(8,128)(2,1)} fusion(f32[512,2048]{1,0:T(8,128)} %fusion.31, bf16[2048,1280]{0,1:T(8,128)(2,1)} %all-gather.5.cloned.1.call-done, f32[512,1024]{1,0:T(8,128)} %copy-done.2, f32[512]{0:T(512)S(1)} %get-tuple-element.397, s32[1024]{0:T(1024)S(1)} %get-tuple-element.402, s32[1024]{0:T(1024)S(1)} %get-tuple-element.401, ...), kind=kOutput, calls=%fused_computation.55 | convolution fusion | flops 811204608 | bytes 10506240 | tf_op jit(solution)/shard_map/th,dh->td/dot_general | solution.py:200
  435.7 73.7 %reduce-scatter.2.cloned.1.call-done = bf16[512,256]{1,0:T(8,128)(2,1)} async-done(((bf16[512,2048]{1,0:T(8,128)(2,1)}), bf16[512,256]{1,0:T(8,128)(2,1)}) %reduce-scatter.2.cloned.1.call-update) | async-done | bytes 262160 | tf_op jit(solution)/shard_map/reduce_scatter | solution.py:203
  509.4 1.8 add_convert_fusion.1
  (244 shorter events, 63.2 us)
Async XLA Ops:
  7.2 3.2 copy-start.6
  7.2 232.2 %all-gather.3.cloned.1.call-start = ((), (), s32[]{:S(2)}) async-start(), calls=%async_computation.2 | async-start | bytes 7798784 | tf_op jit(solution)/shard_map/all_gather | solution.py:139
  16.4 6.8 %copy-start.9 = (bf16[1024,128]{1,0:T(8,128)(2,1)S(1)}, bf16[1024,128]{1,0:T(8,128)(2,1)}, u32[]{:S(2)}) copy-start(bf16[1024,128]{1,0:T(8,128)(2,1)} %param.20) | copy-start | bytes 786436
  16.4 6.8 %copy-start.11 = (bf16[256,128]{1,0:T(8,128)(2,1)S(1)}, bf16[256,128]{1,0:T(8,128)(2,1)}, u32[]{:S(2)}) copy-start(bf16[256,128]{1,0:T(8,128)(2,1)} %param.19) | copy-start | bytes 196612
  16.5 7.7 %copy-start.12 = (s32[64]{0:T(128)S(1)}, s32[64]{0:T(128)}, u32[]{:S(2)}) copy-start(s32[64]{0:T(128)} %param.22) | copy-start | bytes 772
  16.5 8.5 %copy-start.13 = (s32[64]{0:T(128)S(1)}, s32[64]{0:T(128)}, u32[]{:S(2)}) copy-start(s32[64]{0:T(128)} %param.24) | copy-start | bytes 772
  16.5 8.4 %copy-start.14 = (s32[64]{0:T(128)S(1)}, s32[64]{0:T(128)}, u32[]{:S(2)}) copy-start(s32[64]{0:T(128)} %param.23) | copy-start | bytes 772
  16.5 9.5 %copy-start = (bf16[512,2048]{1,0:T(8,128)(2,1)S(1)}, bf16[512,2048]{1,0:T(8,128)(2,1)}, u32[]{:S(2)}) copy-start(bf16[512,2048]{1,0:T(8,128)(2,1)} %param.14) | copy-start | bytes 6291460
  16.5 305.7 %all-to-all-start = ((bf16[16,8,128,2,256]{4,2,1,3,0:T(8,128)(2,1)}), bf16[16,8,128,2,256]{4,2,1,3,0:T(8,128)(2,1)}, u32[]{:S(2)}, u32[]{:S(2)}) async-start(bf16[16,8,128,2,256]{4,2,1,3,0:T(8,128)(2,1)} %stack.4), calls=%async_computation | async-start | bytes 33554432 | tf_op jit(solution)/shard_map/all_to_all | solution.py:179
  23.2 278.5 %all-gather.5.cloned.1.call-start = ((), (), s32[]{:S(2)}) async-start(), calls=%async_computation.3 | async-start | bytes 5570560 | tf_op jit(solution)/shard_map/all_gather | solution.py:199
  24.0 485.3 %reduce-scatter.2.cloned.1.call-start = ((), (), s32[]{:S(2)}) async-start(), calls=%async_computation.4 | async-start | bytes 2359296 | tf_op jit(solution)/shard_map/reduce_scatter | solution.py:203
  239.4 1.9 slice-start
  241.3 3.0 copy-start.15
  248.9 52.8 %copy-start.1 = (bf16[512,2048]{1,0:T(8,128)(2,1)S(1)}, bf16[512,2048]{1,0:T(8,128)(2,1)}, u32[]{:S(2)}) copy-start(bf16[512,2048]{1,0:T(8,128)(2,1)} %param.14) | copy-start | bytes 6291460
  248.9 52.8 %copy-start.16 = (f32[2048]{0:T(1024)S(1)}, f32[2048]{0:T(1024)}, u32[]{:S(2)}) copy-start(f32[2048]{0:T(1024)} %param.16) | copy-start | bytes 24580
  251.2 66.7 %collective-permute-start = (bf16[512,2,256]{0,2,1:T(8,128)(2,1)}, bf16[512,2,256]{0,2,1:T(8,128)(2,1)}, u32[]{:S(2)}, u32[]{:S(2)}) collective-permute-start(bf16[512,2,256]{0,2,1:T(8,128)(2,1)} %pad_maximum_fusion), channel_id=1, source_target_pairs={{0,8},{8,16},{16,24},{24,32},{32,40},{40,48},{48,56},{56,64},{64,7... | collective-permute-start | bytes 1572872 | tf_op jit(solution)/shard_map/ppermute | solution.py:18
  316.0 1.9 copy-start.4
  316.0 3.1 copy-start.8
  322.2 14.2 %copy-start.17 = (s32[128]{0:T(128)S(1)}, s32[128]{0:T(128)}, u32[]{:S(2)}) copy-start(s32[128]{0:T(128)} %param.25) | copy-start | bytes 1540
  336.4 1.6 copy-start.10
  341.1 1.6 copy-start.10
  346.9 1.6 copy-start.10
  352.7 1.6 copy-start.10
  358.4 1.6 copy-start.10
  364.2 1.6 copy-start.10
  369.9 1.6 copy-start.10
  375.7 1.6 copy-start.10
  381.5 1.6 copy-start.10
  387.2 1.6 copy-start.10
  393.0 1.6 copy-start.10
  398.7 1.6 copy-start.10
  404.5 1.6 copy-start.10
  (7 other events, 9.6 us)
Sparse Core Ops, SparseCore 0:
  10.4 228.9 all-gather.2
  241.0 60.5 all-gather.4
  434.0 75.2 reduce-scatter.1
